TPU v7x, 256 devices: a whole 4x4x8 slice. The times are simulated.
256 devices in a mesh: tile: 32 (over x, z), ens: 8 (over y, core).
Axes of the slice: x: 4, y: 4, z: 8, core: 2. Of those that a mesh axis runs over, the one named last changes fastest.
Arguments:
- initial_sample_set: float32 [80, 2, 128, 2048], P('ens', None, 'tile'), may hold values from -6 to 6
- flow_velocity: float32 [2, 2, 128, 2048], P(None, None, 'tile'), may hold values from -0.4 to 0.4
- obs_loc: int32 [3, 2, 32768], P(None, None, 'tile'), may hold values from 0 to 2047, as said below
- obs_count: int32 [2, 32], P(None, 'tile'), may hold values from 256 to 1024, as said below
- obs_value: float32 [2, 32768], P(None, 'tile'), may hold values from -6 to 6
- obs_error: float32 [2, 32768], P(None, 'tile'), may hold values from 0.25 to 2
Outputs:
- analysis: float32 [80, 2, 128, 2048], P('ens', None, 'tile')
Inputs may be any that keep to these rules, and one draw needn't show every extreme that they name: `obs_loc`: slots 1024 * t to 1024 * (t + 1) - 1 of a batch belong to tile t: their row lies in rows 4 * t to 4 * (t + 1) - 1; columns lie in 0 to 2047 and levels in 0 to 1. `obs_count`: in every batch some tile has exactly 1024 live observations; a tile's live observations are its first slots.
All inputs are finite; a program needn't handle non-finite values.
Results may differ from a plain program's by a relative error of at most 0.0003.
Values sent between devices are 32-bit elements; how exact they have to be, the bound alone decides.
A program may use at most 128 MiB of HBM per device.

v0:
```python
import jax
import jax.numpy as jnp
from jax import lax
from jax.sharding import PartitionSpec as P

BATCHES = 2
REACH = 2
SPREAD_RATE = 0.05
EPSILON = 1e-06
PRECISE = lax.Precision.HIGHEST


def with_halo(cells, sides, width):
    for axis, dim in sides:
        count = lax.axis_size(axis)
        ends = count - 1
        head = lax.slice_in_dim(cells, 0, width, axis=dim)
        tail = lax.slice_in_dim(cells, cells.shape[dim] - width, cells.shape[dim], axis=dim)
        cells = jnp.concatenate(
            [
                lax.ppermute(tail, axis, [(i, (i + 1) % count) for i in range(ends)]),
                cells,
                lax.ppermute(head, axis, [((i + 1) % count, i) for i in range(ends)]),
            ],
            axis=dim,
        )
    return cells


def shifted(value, axis, steps):
    count = lax.axis_size(axis)
    leading, last = (max(0, -steps), min(count, count - steps))
    return lax.ppermute(value, axis, [(source, source + steps) for source in range(leading, last)])


def advance(centre, row_above, row_below, col_left, col_right, flow_velocity):
    wind_rows = flow_velocity[0][None]
    wind_cols = flow_velocity[1][None]
    tendency = (
        jnp.maximum(wind_rows, 0.0) * (centre - row_above)
        + jnp.minimum(wind_rows, 0.0) * (row_below - centre)
        + jnp.maximum(wind_cols, 0.0) * (centre - col_left)
        + jnp.minimum(wind_cols, 0.0) * (col_right - centre)
    )
    return (
        centre
        - tendency
        + SPREAD_RATE * (row_above + row_below + col_left + col_right - 4.0 * centre)
    )


def increments(prior_obs, row_values, error_row, live_mask):
    members = prior_obs.shape[0]
    average = jnp.sum(prior_obs, axis=0) / members
    deviation = prior_obs - average[None, :]
    var_prior = jnp.sum(deviation * deviation, axis=0) / (members - 1) + EPSILON
    combined = var_prior + error_row
    shrink_factor = jnp.sqrt(error_row / combined)
    mean_post = (error_row * average + var_prior * row_values) / combined
    obs_shift = live_mask[None, :] * (
        (shrink_factor - 1.0)[None, :] * deviation + (mean_post - average)[None, :]
    )
    weight = live_mask[None, :] * deviation / ((members - 1) * var_prior)[None, :]
    return (weight, obs_shift)


def block_gain(
    states, weight, obs_shift, obs_place, cell_lev, cell_row, cell_col, radius, col_radius
):
    covariance = lax.dot_general(
        weight,
        states,
        (((0,), (0,)), ((), ())),
        precision=PRECISE,
        preferred_element_type=jnp.float32,
    )
    row_gap = cell_row[None, :] - obs_place[0][:, None]
    column_spacing = cell_col[None, :] - obs_place[1][:, None]
    level_gap = jnp.abs(cell_lev[None, :] - obs_place[2][:, None])
    closeness = jnp.maximum(
        1.0
        - row_gap * row_gap / (radius * radius)
        - column_spacing * column_spacing / (col_radius * col_radius),
        0.0,
    )
    gain_map = covariance * (closeness * closeness / (1.0 + level_gap))
    return jnp.dot(obs_shift, gain_map, precision=PRECISE, preferred_element_type=jnp.float32)


def propagate_model(initial_sample_set, flow_velocity):
    padded = with_halo(initial_sample_set, (("tile", 2),), 1)
    padded = jnp.pad(padded, ((0, 0), (0, 0), (0, 0), (1, 1)))
    return advance(
        padded[:, :, 1:-1, 1:-1],
        padded[:, :, :-2, 1:-1],
        padded[:, :, 2:, 1:-1],
        padded[:, :, 1:-1, :-2],
        padded[:, :, 1:-1, 2:],
        flow_velocity,
    )


def analyse(
    columns,
    prior_obs,
    obs_place,
    row_values,
    error_row,
    live_mask,
    cell_lev,
    cell_row,
    cell_col,
    radius,
    col_radius,
):
    weight, obs_shift = increments(prior_obs, row_values, error_row, live_mask)
    payload = (weight, obs_shift, obs_place)
    received = [payload]
    for displacement in range(1, REACH + 1):
        received.append(shifted((payload[0], payload[1], payload[2]), "tile", displacement))
        received.append(shifted((payload[0], payload[1], payload[2]), "tile", -displacement))
    members = columns.shape[0]
    flat_state = columns.reshape(members, -1)
    increment = jnp.zeros_like(flat_state)
    for incoming in received:
        increment = increment + block_gain(
            flat_state,
            incoming[0],
            incoming[1],
            incoming[2],
            cell_lev,
            cell_row,
            cell_col,
            radius,
            col_radius,
        )
    return columns + increment.reshape(columns.shape)


def on_device(initial_sample_set, flow_velocity, obs_loc, obs_count, obs_value, obs_error):
    member_deviation, levels, row_count, col_total = initial_sample_set.shape
    ens_size = lax.axis_size("ens")
    col_count = col_total // ens_size
    obs_tile = obs_value.shape[1]
    tile_index = lax.axis_index("tile")
    ens_index = lax.axis_index("ens")
    radius = float(REACH * row_count)
    col_radius = float(col_total // 2)
    current_model_vector = propagate_model(initial_sample_set, flow_velocity)
    slots = jnp.arange(obs_tile, dtype=jnp.int32)
    cell_index = jnp.arange(levels * row_count * col_count, dtype=jnp.int32)
    cell_lev = (cell_index // (row_count * col_count)).astype(jnp.float32)
    cell_row = (tile_index * row_count + cell_index // col_count % row_count).astype(jnp.float32)
    cell_col = (ens_index * col_count + cell_index % col_count).astype(jnp.float32)
    for batch_index in range(BATCHES):
        local_row = obs_loc[0, batch_index] - tile_index * row_count
        flat_index = (obs_loc[2, batch_index] * row_count + local_row) * col_total + obs_loc[
            1, batch_index
        ]
        own_prior = jnp.take(current_model_vector.reshape(member_deviation, -1), flat_index, axis=1)
        prior_obs = lax.all_gather(own_prior, "ens", axis=0, tiled=True)
        columns = lax.all_to_all(
            current_model_vector, "ens", split_axis=3, concat_axis=0, tiled=True
        )
        live_mask = (slots < obs_count[batch_index, 0]).astype(jnp.float32)
        obs_place = obs_loc[:, batch_index].astype(jnp.float32)
        columns = analyse(
            columns,
            prior_obs,
            obs_place,
            obs_value[batch_index],
            obs_error[batch_index],
            live_mask,
            cell_lev,
            cell_row,
            cell_col,
            radius,
            col_radius,
        )
        current_model_vector = lax.all_to_all(
            columns, "ens", split_axis=0, concat_axis=3, tiled=True
        )
    return current_model_vector


def solution(mesh):
    in_specs = (
        P("ens", None, "tile", None),
        P(None, None, "tile", None),
        P(None, None, "tile"),
        P(None, "tile"),
        P(None, "tile"),
        P(None, "tile"),
    )
    out_specs = P("ens", None, "tile", None)
    return jax.shard_map(
        on_device, mesh=mesh, in_specs=in_specs, out_specs=out_specs, check_vma=False
    )
```

profile of v0, /device:TPU:2, one launch (start us, length us, event | category | flops | bytes accessed | tf_op | source)
XLA Modules:
  0.0 487.8 jit_solution(17337714978346496619)
XLA Ops:
  0.9 8.2 %collective-permute-start.13 = (f32[3,1024]{1,0:T(4,128)S(1)}, f32[3,1024]{1,0:T(4,128)S(1)}, u32[]{:S(2)}, u32[]{:S(2)}) collective-permute-start(f32[3,1024]{1,0:T(4,128)S(1)} %bitcast.143), channel_id=1, source_target_pairs={{16,0},{24,8},{32,16},{40,24},{48,32},{56,40},{64,48},{72,56},{80,... | collective-permute-start | bytes 36872 | tf_op jit(solution)/shard_map/ppermute | solution.py:33
  11.0 6.5 %collective-permute-start.7 = (f32[3,1024]{1,0:T(4,128)S(1)}, f32[3,1024]{1,0:T(4,128)S(1)}, u32[]{:S(2)}, u32[]{:S(2)}) collective-permute-start(f32[3,1024]{1,0:T(4,128)S(1)} %bitcast.145), channel_id=1, source_target_pairs={{8,0},{16,8},{24,16},{32,24},{40,32},{48,40},{56,48},{64,56},{72,6... | collective-permute-start | bytes 36872 | tf_op jit(solution)/shard_map/ppermute | solution.py:33
  19.4 4.4 collective-permute-start.25
  32.5 8.1 %collective-permute-start.19 = (f32[3,1024]{1,0:T(4,128)S(1)}, f32[3,1024]{1,0:T(4,128)S(1)}, u32[]{:S(2)}, u32[]{:S(2)}) collective-permute-start(f32[3,1024]{1,0:T(4,128)S(1)} %bitcast.141), channel_id=1, source_target_pairs={{8,0},{16,8},{24,16},{32,24},{40,32},{48,40},{56,48},{64,56},{72,6... | collective-permute-start | bytes 36872 | tf_op jit(solution)/shard_map/ppermute | solution.py:33
  42.6 6.0 %collective-permute-start.1 = (f32[10,2,1,2048]{3,0,2,1:T(8,128)S(1)}, f32[10,2,1,2048]{3,0,2,1:T(8,128)S(1)}, u32[]{:S(2)}, u32[]{:S(2)}) collective-permute-start(f32[10,2,1,2048]{3,0,2,1:T(8,128)S(1)} %copy.150), channel_id=1, source_target_pairs={{8,0},{16,8},{24,16},{32,24},{40,32},{48,40},{56,48},{64,56},{72,6... | collective-permute-start | bytes 491528 | tf_op jit(solution)/shard_map/ppermute | solution.py:23
  52.7 6.4 %collective-permute-done = f32[10,2,1,2048]{3,0,2,1:T(8,128)S(1)} collective-permute-done((f32[10,2,1,2048]{3,0,2,1:T(8,128)S(1)}, f32[10,2,1,2048]{3,0,2,1:T(8,128)S(1)}, u32[]{:S(2)}, u32[]{:S(2)}) %collective-permute-start) | collective-permute-done | bytes 163872 | tf_op jit(solution)/shard_map/ppermute | solution.py:21
  64.8 4.7 copy.145
  69.5 5.9 %copy.134 = f32[10,2,4,2048]{0,2,1,3:T(4,128)} copy(f32[10,2,4,2048]{3,2,1,0:T(4,128)S(1)} %fusion.291) | data formatting | bytes 1310720 | tf_op jit(solution)/shard_map/add | solution.py:46
  75.5 6.2 %gather_fusion = f32[1024,10]{1,0:T(8,128)S(1)} fusion(f32[10,16384]{0,1:T(8,128)} %bitcast.124, s32[1024]{0:T(1024)S(1)} %fusion.316), kind=kCustom, calls=%fused_computation.clone | custom fusion | bytes 86016 | tf_op jit(solution)/shard_map/jit(_take)/gather | solution.py:160
  82.1 13.6 %all-gather = f32[8,10,1024]{2,1,0:T(8,128)S(1)} all-gather(f32[1,10,1024]{2,1,0:T(8,128)S(1)} %copy.137), channel_id=1, replica_groups=mesh['tile'=32,'ens'=8] {'ens'}, dimensions={0}, use_global_device_ids=true | all-gather | bytes 368640 | tf_op jit(solution)/shard_map/all_gather | solution.py:161
  95.8 12.3 %reshape.233 = f32[8,1,20480]{2,1,0:T(1,128)} reshape(f32[2048,2,4,10]{3,2,1,0:T(4,128)} %bitcast.120) | data formatting | bytes 1310720
  116.1 7.4 %all-to-all-done = f32[8,1,20480]{2,1,0:T(1,128)S(1)} async-done(((f32[8,1,20480]{2,1,0:T(1,128)}), f32[8,1,20480]{2,1,0:T(1,128)S(1)}, u32[]{:S(2)}, u32[]{:S(2)}) %all-to-all-start) | async-done | bytes 655392 | tf_op jit(solution)/shard_map/all_to_all | solution.py:162
  126.3 14.6 %reshape.234 = f32[2048,2,4,10]{3,2,1,0:T(4,128)} reshape(f32[8,20480]{1,0:T(8,128)S(1)} %reduce.2) | data formatting | bytes 1310720
  140.9 7.2 %copy.135 = f32[10,2,4,8,256]{4,2,1,0,3:T(4,128)S(1)} copy(f32[10,2,4,8,256]{0,2,1,4,3:T(4,128)} %bitcast.121) | data formatting | bytes 1310720 | tf_op jit(solution)/shard_map/all_to_all | solution.py:162
  148.5 6.9 %fusion.370 = f32[1024,2048]{1,0:T(8,128)S(1)} fusion(f32[80,1024]{1,0:T(8,128)S(1)} %get-tuple-element.10, f32[80,2048]{1,0:T(8,128)S(1)} %reshape.202), kind=kOutput, calls=%fused_computation.408 | convolution fusion | flops 2013265920 | bytes 9371648 | tf_op jit(solution)/shard_map/dot_general | solution.py:70
  155.4 9.7 %fusion.144 = f32[80,2048]{1,0:T(8,128)S(1)} fusion(f32[80,1024]{1,0:T(8,128)S(1)} %get-tuple-element.11, f32[1024,2048]{1,0:T(8,128)S(1)} %fusion.370, f32[1024]{0:T(1024)S(1)} %bitcast.153, f32[2048]{0:T(1024)S(1)} %get-tuple-element.64, f32[1024]{0:T(1024)S(1)} %bitcast.152, f32[2048]{0:T(1024)S(1)} %fusion.311, f32[1024]{0:T(1024)S(1)} %bitcast.154, ...), kind=kOutput, calls=%fused_computation.146 | convolution fusion | flops 2044723200 | bytes 9408512 | tf_op jit(solution)/shard_map/dot_general | solution.py:87
  167.1 6.9 %fusion.374 = f32[1024,2048]{1,0:T(8,128)S(1)} fusion(f32[80,1024]{1,0:T(8,128)S(1)} %collective-permute-done.12, f32[80,2048]{1,0:T(8,128)S(1)} %reshape.202), kind=kOutput, calls=%fused_computation.412 | convolution fusion | flops 2013265920 | bytes 9371648 | tf_op jit(solution)/shard_map/dot_general | solution.py:70
  176.2 9.6 %fusion.80 = f32[80,2048]{1,0:T(8,128)S(1)} fusion(f32[80,1024]{1,0:T(8,128)S(1)} %collective-permute-done.11, f32[1024,2048]{1,0:T(8,128)S(1)} %fusion.374, f32[1024]{0:T(1024)S(1)} %bitcast.171, f32[1024]{0:T(1024)S(1)} %bitcast.172, f32[1024]{0:T(1024)S(1)} %bitcast.170, f32[2048]{0:T(1024)S(1)} %get-tuple-element.64, f32[2048]{0:T(1024)S(1)} %fusion.311, ...), kind=kOutput, calls=%fused_computation.82 | convolution fusion | flops 2044723200 | bytes 9408512 | tf_op jit(solution)/shard_map/dot_general | solution.py:87
  185.8 13.4 %collective-permute-done.9 = f32[80,1024]{1,0:T(8,128)S(1)} collective-permute-done((f32[80,1024]{1,0:T(8,128)S(1)}, f32[80,1024]{1,0:T(8,128)S(1)}, u32[]{:S(2)}, u32[]{:S(2)}) %collective-permute-start.9) | collective-permute-done | bytes 327712 | tf_op jit(solution)/shard_map/ppermute | solution.py:33
  201.4 6.9 %fusion.373 = f32[1024,2048]{1,0:T(8,128)S(1)} fusion(f32[80,1024]{1,0:T(8,128)S(1)} %collective-permute-done.9, f32[80,2048]{1,0:T(8,128)S(1)} %reshape.202), kind=kOutput, calls=%fused_computation.411 | convolution fusion | flops 2013265920 | bytes 9371648 | tf_op jit(solution)/shard_map/dot_general | solution.py:70
  210.8 9.6 %fusion.96 = f32[80,2048]{1,0:T(8,128)S(1)} fusion(f32[80,1024]{1,0:T(8,128)S(1)} %collective-permute-done.8, f32[1024,2048]{1,0:T(8,128)S(1)} %fusion.373, f32[1024]{0:T(1024)S(1)} %bitcast.165, f32[1024]{0:T(1024)S(1)} %bitcast.166, f32[1024]{0:T(1024)S(1)} %bitcast.164, f32[2048]{0:T(1024)S(1)} %get-tuple-element.64, f32[2048]{0:T(1024)S(1)} %fusion.311, ...), kind=kOutput, calls=%fused_computation.98 | convolution fusion | flops 2044723200 | bytes 9408512 | tf_op jit(solution)/shard_map/dot_general | solution.py:87
  224.4 6.9 %fusion.372 = f32[1024,2048]{1,0:T(8,128)S(1)} fusion(f32[80,1024]{1,0:T(8,128)S(1)} %collective-permute-done.6, f32[80,2048]{1,0:T(8,128)S(1)} %reshape.202), kind=kOutput, calls=%fused_computation.410 | convolution fusion | flops 2013265920 | bytes 9371648 | tf_op jit(solution)/shard_map/dot_general | solution.py:70
  231.3 4.1 collective-permute-start.3
  235.5 9.6 %fusion.112 = f32[80,2048]{1,0:T(8,128)S(1)} fusion(f32[80,1024]{1,0:T(8,128)S(1)} %collective-permute-done.5, f32[1024,2048]{1,0:T(8,128)S(1)} %fusion.372, f32[1024]{0:T(1024)S(1)} %bitcast.162, f32[1024]{0:T(1024)S(1)} %bitcast.163, f32[1024]{0:T(1024)S(1)} %bitcast.161, f32[2048]{0:T(1024)S(1)} %get-tuple-element.64, f32[2048]{0:T(1024)S(1)} %fusion.311, ...), kind=kOutput, calls=%fused_computation.114 | convolution fusion | flops 2044723200 | bytes 9408512 | tf_op jit(solution)/shard_map/dot_general | solution.py:87
  245.0 7.3 %fusion.371 = f32[1024,2048]{1,0:T(8,128)S(1)} fusion(f32[80,1024]{1,0:T(8,128)S(1)} %collective-permute-done.3, f32[80,2048]{1,0:T(8,128)S(1)} %reshape.202), kind=kOutput, calls=%fused_computation.409 | convolution fusion | flops 2013265920 | bytes 9371648 | tf_op jit(solution)/shard_map/dot_general | solution.py:70
  252.4 9.8 %fusion.269 = f32[80,2048]{1,0:T(8,128)S(1)} fusion(f32[80,2048]{1,0:T(8,128)S(1)} %fusion.80, f32[80,2048]{1,0:T(8,128)S(1)} %fusion.96, f32[80,2048]{1,0:T(8,128)S(1)} %fusion.112, f32[80,2048]{1,0:T(8,128)S(1)} %fusion.144, f32[80,1024]{1,0:T(8,128)S(1)} %collective-permute-done.2, f32[1024,2048]{1,0:T(8,128)S(1)} %fusion.371, f32[1024]{0:T(1024)S(1)} %bitcast.159, ...), kind=kOutput, calls=%fused_computation.265 | convolution fusion | flops 2045378560 | bytes 12029952 | tf_op jit(solution)/shard_map/dot_general | solution.py:87
  267.3 11.6 %all-to-all-done.1 = f32[80,2,4,256]{3,2,1,0:T(4,128)S(1)} async-done(((f32[80,2,4,256]{3,2,1,0:T(4,128)}), f32[80,2,4,256]{3,2,1,0:T(4,128)S(1)}, u32[]{:S(2)}, u32[]{:S(2)}) %all-to-all-start.1) | async-done | bytes 655392 | tf_op jit(solution)/shard_map/all_to_all | solution.py:180
  278.9 4.7 copy.138
  283.6 6.2 %gather_fusion.1 = f32[1024,10]{1,0:T(8,128)S(1)} fusion(f32[10,16384]{0,1:T(8,128)} %bitcast.118, s32[1024]{0:T(1024)S(1)} %fusion.317), kind=kCustom, calls=%fused_computation.1.clone | custom fusion | bytes 86016 | tf_op jit(solution)/shard_map/jit(_take)/gather | solution.py:160
  290.2 13.1 %all-gather.1 = f32[8,10,1024]{2,1,0:T(8,128)S(1)} all-gather(f32[1,10,1024]{2,1,0:T(8,128)S(1)} %copy.142), channel_id=1, replica_groups=mesh['tile'=32,'ens'=8] {'ens'}, dimensions={0}, use_global_device_ids=true | all-gather | bytes 368640 | tf_op jit(solution)/shard_map/all_gather | solution.py:161
  303.4 12.0 %copy.139 = f32[10,2,4,8,256]{0,2,1,4,3:T(4,128)} copy(f32[10,2,4,8,256]{0,4,3,2,1:T(8,128)} %bitcast.119) | data formatting | bytes 1310720 | tf_op jit(solution)/shard_map/all_to_all | solution.py:180
  315.4 12.2 %reshape.235 = f32[8,1,20480]{2,1,0:T(1,128)} reshape(f32[2048,2,4,10]{3,2,1,0:T(4,128)} %bitcast.122) | data formatting | bytes 1310720
  338.2 5.7 %collective-permute-start.24 = (f32[80,1024]{1,0:T(8,128)S(1)}, f32[80,1024]{1,0:T(8,128)S(1)}, u32[]{:S(2)}, u32[]{:S(2)}) collective-permute-start(f32[80,1024]{1,0:T(8,128)S(1)} %get-tuple-element.8), channel_id=1, source_target_pairs={{16,0},{24,8},{32,16},{40,24},{48,32},{56,40},{64,48},{72,56},{80,... | collective-permute-start | bytes 983048 | tf_op jit(solution)/shard_map/ppermute | solution.py:33
  345.8 7.6 %collective-permute-start.17 = (f32[80,1024]{1,0:T(8,128)S(1)}, f32[80,1024]{1,0:T(8,128)S(1)}, u32[]{:S(2)}, u32[]{:S(2)}) collective-permute-start(f32[80,1024]{1,0:T(8,128)S(1)} %get-tuple-element.9), channel_id=1, source_target_pairs={{8,0},{16,8},{24,16},{32,24},{40,32},{48,40},{56,48},{64,56},{72,6... | collective-permute-start | bytes 983048 | tf_op jit(solution)/shard_map/ppermute | solution.py:33
  355.6 14.6 %reshape.236 = f32[2048,2,4,10]{3,2,1,0:T(4,128)} reshape(f32[8,20480]{1,0:T(8,128)S(1)} %reduce.3) | data formatting | bytes 1310720
  370.2 5.7 %copy.146 = f32[10,2,4,8,256]{4,3,2,1,0:T(8,128)S(1)} copy(f32[10,2,4,8,256]{0,2,1,4,3:T(4,128)} %bitcast.123) | data formatting | bytes 1310720 | tf_op jit(solution)/shard_map/all_to_all | solution.py:162
  376.5 6.9 %fusion.375 = f32[1024,2048]{1,0:T(8,128)S(1)} fusion(f32[80,1024]{1,0:T(8,128)S(1)} %get-tuple-element.8, f32[80,2048]{1,0:T(8,128)S(1)} %reshape.205), kind=kOutput, calls=%fused_computation.413 | convolution fusion | flops 2013265920 | bytes 9371648 | tf_op jit(solution)/shard_map/dot_general | solution.py:70
  383.4 9.7 %fusion.64 = f32[80,2048]{1,0:T(8,128)S(1)} fusion(f32[80,1024]{1,0:T(8,128)S(1)} %get-tuple-element.9, f32[1024,2048]{1,0:T(8,128)S(1)} %fusion.375, f32[1024]{0:T(1024)S(1)} %bitcast.150, f32[1024]{0:T(1024)S(1)} %bitcast.151, f32[1024]{0:T(1024)S(1)} %bitcast.149, f32[2048]{0:T(1024)S(1)} %get-tuple-element.64, f32[2048]{0:T(1024)S(1)} %fusion.311, ...), kind=kOutput, calls=%fused_computation.66 | convolution fusion | flops 2044723200 | bytes 9408512 | tf_op jit(solution)/shard_map/dot_general | solution.py:87
  395.2 6.9 %fusion.379 = f32[1024,2048]{1,0:T(8,128)S(1)} fusion(f32[80,1024]{1,0:T(8,128)S(1)} %collective-permute-done.24, f32[80,2048]{1,0:T(8,128)S(1)} %reshape.205), kind=kOutput, calls=%fused_computation.417 | convolution fusion | flops 2013265920 | bytes 9371648 | tf_op jit(solution)/shard_map/dot_general | solution.py:70
  402.2 4.1 collective-permute-start.14
  406.3 10.5 %fusion = f32[80,2048]{1,0:T(8,128)S(1)} fusion(f32[80,1024]{1,0:T(8,128)} %collective-permute-done.23, f32[1024,2048]{1,0:T(8,128)S(1)} %fusion.379, f32[1024]{0:T(1024)S(1)} %bitcast.156, f32[1024]{0:T(1024)S(1)} %bitcast.157, f32[1024]{0:T(1024)S(1)} %bitcast.155, f32[2048]{0:T(1024)S(1)} %get-tuple-element.64, f32[2048]{0:T(1024)S(1)} %fusion.311, ...), kind=kOutput, calls=%fused_computation.2 | convolution fusion | flops 2044723200 | bytes 9408512 | tf_op jit(solution)/shard_map/dot_general | solution.py:87
  419.2 6.9 %fusion.378 = f32[1024,2048]{1,0:T(8,128)S(1)} fusion(f32[80,1024]{1,0:T(8,128)S(1)} %collective-permute-done.21, f32[80,2048]{1,0:T(8,128)S(1)} %reshape.205), kind=kOutput, calls=%fused_computation.416 | convolution fusion | flops 2013265920 | bytes 9371648 | tf_op jit(solution)/shard_map/dot_general | solution.py:70
  426.1 9.7 %fusion.16 = f32[80,2048]{1,0:T(8,128)S(1)} fusion(f32[80,1024]{1,0:T(8,128)S(1)} %collective-permute-done.20, f32[1024,2048]{1,0:T(8,128)S(1)} %fusion.378, f32[1024]{0:T(1024)S(1)} %bitcast.177, f32[1024]{0:T(1024)S(1)} %bitcast.178, f32[1024]{0:T(1024)S(1)} %bitcast.176, f32[2048]{0:T(1024)S(1)} %get-tuple-element.64, f32[2048]{0:T(1024)S(1)} %fusion.311, ...), kind=kOutput, calls=%fused_computation.18 | convolution fusion | flops 2044723200 | bytes 9408512 | tf_op jit(solution)/shard_map/dot_general | solution.py:87
  435.9 6.9 %fusion.377 = f32[1024,2048]{1,0:T(8,128)S(1)} fusion(f32[80,1024]{1,0:T(8,128)S(1)} %collective-permute-done.18, f32[80,2048]{1,0:T(8,128)S(1)} %reshape.205), kind=kOutput, calls=%fused_computation.415 | convolution fusion | flops 2013265920 | bytes 9371648 | tf_op jit(solution)/shard_map/dot_general | solution.py:70
  442.8 9.8 %fusion.32 = f32[80,2048]{1,0:T(8,128)S(1)} fusion(f32[80,1024]{1,0:T(8,128)S(1)} %collective-permute-done.17, f32[1024,2048]{1,0:T(8,128)S(1)} %fusion.377, f32[1024]{0:T(1024)S(1)} %bitcast.174, f32[1024]{0:T(1024)S(1)} %bitcast.175, f32[1024]{0:T(1024)S(1)} %bitcast.173, f32[2048]{0:T(1024)S(1)} %get-tuple-element.64, f32[2048]{0:T(1024)S(1)} %fusion.311, ...), kind=kOutput, calls=%fused_computation.34 | convolution fusion | flops 2044723200 | bytes 9408512 | tf_op jit(solution)/shard_map/dot_general | solution.py:87
  452.6 7.2 %fusion.376 = f32[1024,2048]{1,0:T(8,128)S(1)} fusion(f32[80,1024]{1,0:T(8,128)S(1)} %collective-permute-done.15, f32[80,2048]{1,0:T(8,128)S(1)} %reshape.205), kind=kOutput, calls=%fused_computation.414 | convolution fusion | flops 2013265920 | bytes 9371648 | tf_op jit(solution)/shard_map/dot_general | solution.py:70
  459.8 9.7 %fusion.281 = f32[80,2048]{1,0:T(8,128)S(1)} fusion(f32[80,2048]{1,0:T(8,128)S(1)} %fusion, f32[80,2048]{1,0:T(8,128)S(1)} %fusion.16, f32[80,2048]{1,0:T(8,128)S(1)} %fusion.32, f32[80,2048]{1,0:T(8,128)S(1)} %fusion.64, f32[80,1024]{1,0:T(8,128)S(1)} %collective-permute-done.14, f32[1024,2048]{1,0:T(8,128)S(1)} %fusion.376, f32[1024]{0:T(1024)S(1)} %bitcast.168, ...), kind=kOutput, calls=%fused_computation.269 | convolution fusion | flops 2045378560 | bytes 12029952 | tf_op jit(solution)/shard_map/dot_general | solution.py:87
  470.1 16.3 %all_to_all.72 = f32[80,2,4,256]{3,2,1,0:T(4,128)S(1)} all-to-all(f32[80,2,4,256]{3,2,1,0:T(4,128)S(1)} %bitcast_add_fusion.1), channel_id=1, replica_groups=mesh['tile'=32,'ens'=8] {'ens'}, dimensions={0} | all-to-all | bytes 1310720 | tf_op jit(solution)/shard_map/all_to_all | solution.py:180
  (114 shorter events, 75.9 us)
Async XLA Ops:
  0.9 29.2 %collective-permute-start.13 = (f32[3,1024]{1,0:T(4,128)S(1)}, f32[3,1024]{1,0:T(4,128)S(1)}, u32[]{:S(2)}, u32[]{:S(2)}) collective-permute-start(f32[3,1024]{1,0:T(4,128)S(1)} %bitcast.143), channel_id=1, source_target_pairs={{16,0},{24,8},{32,16},{40,24},{48,32},{56,40},{64,48},{72,56},{80,... | collective-permute-start | bytes 36872 | tf_op jit(solution)/shard_map/ppermute | solution.py:33
  9.0 23.5 %collective-permute-start.10 = (f32[3,1024]{1,0:T(4,128)S(1)}, f32[3,1024]{1,0:T(4,128)S(1)}, u32[]{:S(2)}, u32[]{:S(2)}) collective-permute-start(f32[3,1024]{1,0:T(4,128)S(1)} %bitcast.144), channel_id=1, source_target_pairs={{0,16},{8,24},{16,32},{24,40},{32,48},{40,56},{48,64},{56,72},{64,... | collective-permute-start | bytes 36872 | tf_op jit(solution)/shard_map/ppermute | solution.py:33
  11.0 29.7 %collective-permute-start.7 = (f32[3,1024]{1,0:T(4,128)S(1)}, f32[3,1024]{1,0:T(4,128)S(1)}, u32[]{:S(2)}, u32[]{:S(2)}) collective-permute-start(f32[3,1024]{1,0:T(4,128)S(1)} %bitcast.145), channel_id=1, source_target_pairs={{8,0},{16,8},{24,16},{32,24},{40,32},{48,40},{56,48},{64,56},{72,6... | collective-permute-start | bytes 36872 | tf_op jit(solution)/shard_map/ppermute | solution.py:33
  17.5 25.2 %collective-permute-start.4 = (f32[3,1024]{1,0:T(4,128)S(1)}, f32[3,1024]{1,0:T(4,128)S(1)}, u32[]{:S(2)}, u32[]{:S(2)}) collective-permute-start(f32[3,1024]{1,0:T(4,128)S(1)} %bitcast.146), channel_id=1, source_target_pairs={{0,8},{8,16},{16,24},{24,32},{32,40},{40,48},{48,56},{56,64},{64,7... | collective-permute-start | bytes 36872 | tf_op jit(solution)/shard_map/ppermute | solution.py:33
  19.4 29.3 %collective-permute-start.25 = (f32[3,1024]{1,0:T(4,128)S(1)}, f32[3,1024]{1,0:T(4,128)S(1)}, u32[]{:S(2)}, u32[]{:S(2)}) collective-permute-start(f32[3,1024]{1,0:T(4,128)S(1)} %bitcast.139), channel_id=1, source_target_pairs={{16,0},{24,8},{32,16},{40,24},{48,32},{56,40},{64,48},{72,56},{80,... | collective-permute-start | bytes 36872 | tf_op jit(solution)/shard_map/ppermute | solution.py:33
  30.1 237.2 %collective-permute-start.22 = (f32[3,1024]{1,0:T(4,128)S(1)}, f32[3,1024]{1,0:T(4,128)S(1)}, u32[]{:S(2)}, u32[]{:S(2)}) collective-permute-start(f32[3,1024]{1,0:T(4,128)S(1)} %bitcast.140), channel_id=1, source_target_pairs={{0,16},{8,24},{16,32},{24,40},{32,48},{40,56},{48,64},{56,72},{64,... | collective-permute-start | bytes 36872 | tf_op jit(solution)/shard_map/ppermute | solution.py:33
  32.5 234.8 %collective-permute-start.19 = (f32[3,1024]{1,0:T(4,128)S(1)}, f32[3,1024]{1,0:T(4,128)S(1)}, u32[]{:S(2)}, u32[]{:S(2)}) collective-permute-start(f32[3,1024]{1,0:T(4,128)S(1)} %bitcast.141), channel_id=1, source_target_pairs={{8,0},{16,8},{24,16},{32,24},{40,32},{48,40},{56,48},{64,56},{72,6... | collective-permute-start | bytes 36872 | tf_op jit(solution)/shard_map/ppermute | solution.py:33
  40.7 226.6 %collective-permute-start.16 = (f32[3,1024]{1,0:T(4,128)S(1)}, f32[3,1024]{1,0:T(4,128)S(1)}, u32[]{:S(2)}, u32[]{:S(2)}) collective-permute-start(f32[3,1024]{1,0:T(4,128)S(1)} %bitcast.142), channel_id=1, source_target_pairs={{0,8},{8,16},{16,24},{24,32},{32,40},{40,48},{48,56},{56,64},{64,7... | collective-permute-start | bytes 36872 | tf_op jit(solution)/shard_map/ppermute | solution.py:33
  42.6 9.9 %collective-permute-start.1 = (f32[10,2,1,2048]{3,0,2,1:T(8,128)S(1)}, f32[10,2,1,2048]{3,0,2,1:T(8,128)S(1)}, u32[]{:S(2)}, u32[]{:S(2)}) collective-permute-start(f32[10,2,1,2048]{3,0,2,1:T(8,128)S(1)} %copy.150), channel_id=1, source_target_pairs={{8,0},{16,8},{24,16},{32,24},{40,32},{48,40},{56,48},{64,56},{72,6... | collective-permute-start | bytes 491528 | tf_op jit(solution)/shard_map/ppermute | solution.py:23
  48.7 10.4 %collective-permute-start = (f32[10,2,1,2048]{3,0,2,1:T(8,128)S(1)}, f32[10,2,1,2048]{3,0,2,1:T(8,128)S(1)}, u32[]{:S(2)}, u32[]{:S(2)}) collective-permute-start(f32[10,2,1,2048]{3,0,2,1:T(8,128)S(1)} %copy.149), channel_id=1, source_target_pairs={{0,8},{8,16},{16,24},{24,32},{32,40},{40,48},{48,56},{56,64},{64,7... | collective-permute-start | bytes 491528 | tf_op jit(solution)/shard_map/ppermute | solution.py:21
  75.5 36.4 %copy-start = (f32[2,1024]{1,0:T(2,128)S(1)}, f32[2,1024]{1,0:T(2,128)}, u32[]{:S(2)}) copy-start(f32[2,1024]{1,0:T(2,128)} %param.13) | copy-start | bytes 24580
  75.5 36.5 %copy-start.1 = (f32[2,1024]{1,0:T(2,128)S(1)}, f32[2,1024]{1,0:T(2,128)}, u32[]{:S(2)}) copy-start(f32[2,1024]{1,0:T(2,128)} %param.12) | copy-start | bytes 24580
  108.1 15.5 %all-to-all-start = ((f32[8,1,20480]{2,1,0:T(1,128)}), f32[8,1,20480]{2,1,0:T(1,128)S(1)}, u32[]{:S(2)}, u32[]{:S(2)}) async-start(f32[8,1,20480]{2,1,0:T(1,128)} %reshape.233), calls=%async_computation | async-start | bytes 1310720 | tf_op jit(solution)/shard_map/all_to_all | solution.py:162
  112.1 62.0 %collective-permute-start.11 = (f32[80,1024]{1,0:T(8,128)S(1)}, f32[80,1024]{1,0:T(8,128)S(1)}, u32[]{:S(2)}, u32[]{:S(2)}) collective-permute-start(f32[80,1024]{1,0:T(8,128)S(1)} %get-tuple-element.11), channel_id=1, source_target_pairs={{16,0},{24,8},{32,16},{40,24},{48,32},{56,40},{64,48},{72,56},{80,... | collective-permute-start | bytes 983048 | tf_op jit(solution)/shard_map/ppermute | solution.py:33
  114.0 51.2 %collective-permute-start.12 = (f32[80,1024]{1,0:T(8,128)S(1)}, f32[80,1024]{1,0:T(8,128)S(1)}, u32[]{:S(2)}, u32[]{:S(2)}) collective-permute-start(f32[80,1024]{1,0:T(8,128)S(1)} %get-tuple-element.10), channel_id=1, source_target_pairs={{16,0},{24,8},{32,16},{40,24},{48,32},{56,40},{64,48},{72,56},{80,... | collective-permute-start | bytes 983048 | tf_op jit(solution)/shard_map/ppermute | solution.py:33
  165.2 43.2 %collective-permute-start.8 = (f32[80,1024]{1,0:T(8,128)S(1)}, f32[80,1024]{1,0:T(8,128)S(1)}, u32[]{:S(2)}, u32[]{:S(2)}) collective-permute-start(f32[80,1024]{1,0:T(8,128)S(1)} %get-tuple-element.11), channel_id=1, source_target_pairs={{0,16},{8,24},{16,32},{24,40},{32,48},{40,56},{48,64},{56,72},{64,... | collective-permute-start | bytes 983048 | tf_op jit(solution)/shard_map/ppermute | solution.py:33
  174.1 25.1 %collective-permute-start.9 = (f32[80,1024]{1,0:T(8,128)S(1)}, f32[80,1024]{1,0:T(8,128)S(1)}, u32[]{:S(2)}, u32[]{:S(2)}) collective-permute-start(f32[80,1024]{1,0:T(8,128)S(1)} %get-tuple-element.10), channel_id=1, source_target_pairs={{0,16},{8,24},{16,32},{24,40},{32,48},{40,56},{48,64},{56,72},{64,... | collective-permute-start | bytes 983048 | tf_op jit(solution)/shard_map/ppermute | solution.py:33
  199.2 32.1 %collective-permute-start.5 = (f32[80,1024]{1,0:T(8,128)S(1)}, f32[80,1024]{1,0:T(8,128)S(1)}, u32[]{:S(2)}, u32[]{:S(2)}) collective-permute-start(f32[80,1024]{1,0:T(8,128)S(1)} %get-tuple-element.11), channel_id=1, source_target_pairs={{8,0},{16,8},{24,16},{32,24},{40,32},{48,40},{56,48},{64,56},{72,6... | collective-permute-start | bytes 983048 | tf_op jit(solution)/shard_map/ppermute | solution.py:33
  208.3 12.0 %collective-permute-start.6 = (f32[80,1024]{1,0:T(8,128)S(1)}, f32[80,1024]{1,0:T(8,128)S(1)}, u32[]{:S(2)}, u32[]{:S(2)}) collective-permute-start(f32[80,1024]{1,0:T(8,128)S(1)} %get-tuple-element.10), channel_id=1, source_target_pairs={{8,0},{16,8},{24,16},{32,24},{40,32},{48,40},{56,48},{64,56},{72,6... | collective-permute-start | bytes 983048 | tf_op jit(solution)/shard_map/ppermute | solution.py:33
  220.4 32.0 %collective-permute-start.2 = (f32[80,1024]{1,0:T(8,128)S(1)}, f32[80,1024]{1,0:T(8,128)S(1)}, u32[]{:S(2)}, u32[]{:S(2)}) collective-permute-start(f32[80,1024]{1,0:T(8,128)S(1)} %get-tuple-element.11), channel_id=1, source_target_pairs={{0,8},{8,16},{16,24},{24,32},{32,40},{40,48},{48,56},{56,64},{64,7... | collective-permute-start | bytes 983048 | tf_op jit(solution)/shard_map/ppermute | solution.py:33
  231.3 13.7 %collective-permute-start.3 = (f32[80,1024]{1,0:T(8,128)S(1)}, f32[80,1024]{1,0:T(8,128)S(1)}, u32[]{:S(2)}, u32[]{:S(2)}) collective-permute-start(f32[80,1024]{1,0:T(8,128)S(1)} %get-tuple-element.10), channel_id=1, source_target_pairs={{0,8},{8,16},{16,24},{24,32},{32,40},{40,48},{48,56},{56,64},{64,7... | collective-permute-start | bytes 983048 | tf_op jit(solution)/shard_map/ppermute | solution.py:33
  263.7 15.2 %all-to-all-start.1 = ((f32[80,2,4,256]{3,2,1,0:T(4,128)}), f32[80,2,4,256]{3,2,1,0:T(4,128)S(1)}, u32[]{:S(2)}, u32[]{:S(2)}) async-start(f32[80,2,4,256]{3,2,1,0:T(4,128)} %bitcast_add_fusion), calls=%async_computation.1 | async-start | bytes 1310720 | tf_op jit(solution)/shard_map/all_to_all | solution.py:180
  327.7 25.8 %all-to-all-start.2 = ((f32[8,1,20480]{2,1,0:T(1,128)}), f32[8,1,20480]{2,1,0:T(1,128)S(1)}, u32[]{:S(2)}, u32[]{:S(2)}) async-start(f32[8,1,20480]{2,1,0:T(1,128)} %reshape.235), calls=%async_computation.2 | async-start | bytes 1310720 | tf_op jit(solution)/shard_map/all_to_all | solution.py:162
  331.4 70.8 %collective-permute-start.23 = (f32[80,1024]{1,0:T(8,128)S(1)}, f32[80,1024]{1,0:T(8,128)}, u32[]{:S(2)}, u32[]{:S(2)}) collective-permute-start(f32[80,1024]{1,0:T(8,128)S(1)} %get-tuple-element.9), channel_id=1, source_target_pairs={{16,0},{24,8},{32,16},{40,24},{48,32},{56,40},{64,48},{72,56},{80,... | collective-permute-start | bytes 983048 | tf_op jit(solution)/shard_map/ppermute | solution.py:33
  335.0 91.1 %collective-permute-start.20 = (f32[80,1024]{1,0:T(8,128)S(1)}, f32[80,1024]{1,0:T(8,128)S(1)}, u32[]{:S(2)}, u32[]{:S(2)}) collective-permute-start(f32[80,1024]{1,0:T(8,128)S(1)} %get-tuple-element.9), channel_id=1, source_target_pairs={{0,16},{8,24},{16,32},{24,40},{32,48},{40,56},{48,64},{56,72},{64,... | collective-permute-start | bytes 983048 | tf_op jit(solution)/shard_map/ppermute | solution.py:33
  338.2 55.0 %collective-permute-start.24 = (f32[80,1024]{1,0:T(8,128)S(1)}, f32[80,1024]{1,0:T(8,128)S(1)}, u32[]{:S(2)}, u32[]{:S(2)}) collective-permute-start(f32[80,1024]{1,0:T(8,128)S(1)} %get-tuple-element.8), channel_id=1, source_target_pairs={{16,0},{24,8},{32,16},{40,24},{48,32},{56,40},{64,48},{72,56},{80,... | collective-permute-start | bytes 983048 | tf_op jit(solution)/shard_map/ppermute | solution.py:33
  343.9 73.0 %collective-permute-start.21 = (f32[80,1024]{1,0:T(8,128)S(1)}, f32[80,1024]{1,0:T(8,128)S(1)}, u32[]{:S(2)}, u32[]{:S(2)}) collective-permute-start(f32[80,1024]{1,0:T(8,128)S(1)} %get-tuple-element.8), channel_id=1, source_target_pairs={{0,16},{8,24},{16,32},{24,40},{32,48},{40,56},{48,64},{56,72},{64,... | collective-permute-start | bytes 983048 | tf_op jit(solution)/shard_map/ppermute | solution.py:33
  345.8 97.0 %collective-permute-start.17 = (f32[80,1024]{1,0:T(8,128)S(1)}, f32[80,1024]{1,0:T(8,128)S(1)}, u32[]{:S(2)}, u32[]{:S(2)}) collective-permute-start(f32[80,1024]{1,0:T(8,128)S(1)} %get-tuple-element.9), channel_id=1, source_target_pairs={{8,0},{16,8},{24,16},{32,24},{40,32},{48,40},{56,48},{64,56},{72,6... | collective-permute-start | bytes 983048 | tf_op jit(solution)/shard_map/ppermute | solution.py:33
  393.2 13.1 %copy-start.2 = (f32[1,1024]{1,0:T(1,128)S(1)}, f32[1,1024]{1,0:T(1,128)}, u32[]{:S(2)}) copy-start(f32[1,1024]{1,0:T(1,128)} %get-tuple-element.29) | copy-start | bytes 12292
  393.2 13.1 %copy-start.3 = (f32[1,1024]{1,0:T(1,128)S(1)}, f32[1,1024]{1,0:T(1,128)}, u32[]{:S(2)}) copy-start(f32[1,1024]{1,0:T(1,128)} %get-tuple-element.30) | copy-start | bytes 12292
  393.2 13.1 %copy-start.4 = (f32[1,1024]{1,0:T(1,128)S(1)}, f32[1,1024]{1,0:T(1,128)}, u32[]{:S(2)}) copy-start(f32[1,1024]{1,0:T(1,128)} %get-tuple-element.31) | copy-start | bytes 12292
  393.2 42.6 %collective-permute-start.18 = (f32[80,1024]{1,0:T(8,128)S(1)}, f32[80,1024]{1,0:T(8,128)S(1)}, u32[]{:S(2)}, u32[]{:S(2)}) collective-permute-start(f32[80,1024]{1,0:T(8,128)S(1)} %get-tuple-element.8), channel_id=1, source_target_pairs={{8,0},{16,8},{24,16},{32,24},{40,32},{48,40},{56,48},{64,56},{72,6... | collective-permute-start | bytes 983048 | tf_op jit(solution)/shard_map/ppermute | solution.py:33
  402.2 57.6 %collective-permute-start.14 = (f32[80,1024]{1,0:T(8,128)S(1)}, f32[80,1024]{1,0:T(8,128)S(1)}, u32[]{:S(2)}, u32[]{:S(2)}) collective-permute-start(f32[80,1024]{1,0:T(8,128)S(1)} %get-tuple-element.9), channel_id=1, source_target_pairs={{0,8},{8,16},{16,24},{24,32},{32,40},{40,48},{48,56},{56,64},{64,7... | collective-permute-start | bytes 983048 | tf_op jit(solution)/shard_map/ppermute | solution.py:33
  416.8 35.8 %collective-permute-start.15 = (f32[80,1024]{1,0:T(8,128)S(1)}, f32[80,1024]{1,0:T(8,128)S(1)}, u32[]{:S(2)}, u32[]{:S(2)}) collective-permute-start(f32[80,1024]{1,0:T(8,128)S(1)} %get-tuple-element.8), channel_id=1, source_target_pairs={{0,8},{8,16},{16,24},{24,32},{32,40},{40,48},{48,56},{56,64},{64,7... | collective-permute-start | bytes 983048 | tf_op jit(solution)/shard_map/ppermute | solution.py:33
where the time goes:
time: 496 us; the launch traced here: 488 us
  matrix products  168 us (34%)
  local copies, waits for them, and re-layouts  114 us (23%)
  starting transfers between devices  105 us (21%)
  blocking collectives  43 us (9%)
  waiting for transfers between devices  40.2 us (8%)
  other arithmetic  15.9 us (3%)
    dot_general x10, matrix products, block_gain(): jnp.dot(obs_shift, gain_map, precision=PRECISE, preferred_element_type=jn...  97.6 us
    ppermute x24, starting transfers between devices, shifted(): lax.ppermute(value, axis, [(source, source + steps) for source in range(l...  86.5 us
    dot_general x10, matrix products, block_gain(): lax.dot_general(weight, states, (((0,), (0,)), ((), ())), precision=PRECI...  70 us
    unnamed x22, local copies, waits for them, and re-layouts  54.4 us
    all_gather x2, blocking collectives, on_device(): prior_obs = lax.all_gather(own_prior, 'ens', axis=0, tiled=True)  26.7 us
    all_to_all x3, local copies, waits for them, and re-layouts, on_device(): lax.all_to_all(columns, 'ens', split_axis=0, concat_axis=3, tiled=True)  17.7 us
    all_to_all x1, blocking collectives, on_device(): lax.all_to_all(columns, 'ens', split_axis=0, concat_axis=3, tiled=True)  16.3 us
    all_to_all x4, local copies, waits for them, and re-layouts, on_device(): lax.all_to_all(current_model_vector, 'ens', split_axis=3, concat_axis=0,...  13.7 us
  transfers between devices with their start and end apart: 29, of which 5 were waited for; matrix products, arithmetic and copies ran while one was open for 51% of the time, Pallas kernels for 0%

commit v1 on v0

--- a/solution.py
+++ b/solution.py
@@ -158,7 +158,9 @@
             1, batch_index
         ]
         own_prior = jnp.take(current_model_vector.reshape(member_deviation, -1), flat_index, axis=1)
-        prior_obs = lax.all_gather(own_prior, "ens", axis=0, tiled=True)
+        prior_obs = jnp.concatenate(
+            lax.all_to_all(jnp.stack([own_prior] * lax.axis_size("ens")), "ens", 0, 0), axis=0
+        )
         columns = lax.all_to_all(
             current_model_vector, "ens", split_axis=3, concat_axis=0, tiled=True
         )

time: 496 us -> 493 us (level)
  the two profiles are of different devices: /device:TPU:2 before, /device:TPU:6 now
where the time goes in v1:
time: 493 us; the launch traced here: 485 us
  matrix products  169 us (34%)
  starting transfers between devices  117 us (24%)
  local copies, waits for them, and re-layouts  116 us (24%)
  waiting for transfers between devices  48.3 us (10%)
  blocking collectives  16.4 us (3%)
  other arithmetic  16.1 us (3%)
    dot_general x10, matrix products, block_gain(): jnp.dot(obs_shift, gain_map, precision=PRECISE, preferred_element_type=jn...  99.4 us
    ppermute x24, starting transfers between devices, shifted(): lax.ppermute(value, axis, [(source, source + steps) for source in range(l...  88 us
    dot_general x10, matrix products, block_gain(): lax.dot_general(weight, states, (((0,), (0,)), ((), ())), precision=PRECI...  69.6 us
    unnamed x14, local copies, waits for them, and re-layouts  54 us
    ppermute x24, waiting for transfers between devices, shifted(): lax.ppermute(value, axis, [(source, source + steps) for source in range(l...  28 us
    all_to_all x3, local copies, waits for them, and re-layouts, on_device(): lax.all_to_all(columns, 'ens', split_axis=0, concat_axis=3, tiled=True)  17.7 us
    all_to_all x1, blocking collectives, on_device(): lax.all_to_all(columns, 'ens', split_axis=0, concat_axis=3, tiled=True)  16.4 us
    all_to_all x4, local copies, waits for them, and re-layouts, on_device(): lax.all_to_all(current_model_vector, 'ens', split_axis=3, concat_axis=0,...  13.7 us
  transfers between devices with their start and end apart: 31, of which 8 were waited for; matrix products, arithmetic and copies ran while one was open for 60% of the time, Pallas kernels for 0%

profile of v1, /device:TPU:6, one launch (start us, length us, event | category | flops | bytes accessed | tf_op | source)
XLA Modules:
  0.0 484.6 jit_solution(8072913888124517805)
XLA Ops:
  0.9 8.5 %collective-permute-start.13 = (f32[3,1024]{1,0:T(4,128)S(1)}, f32[3,1024]{1,0:T(4,128)S(1)}, u32[]{:S(2)}, u32[]{:S(2)}) collective-permute-start(f32[3,1024]{1,0:T(4,128)S(1)} %bitcast.139), channel_id=1, source_target_pairs={{16,0},{24,8},{32,16},{40,24},{48,32},{56,40},{64,48},{72,56},{80,... | collective-permute-start | bytes 36872 | tf_op jit(solution)/shard_map/ppermute | solution.py:33
  11.3 6.5 %collective-permute-start.7 = (f32[3,1024]{1,0:T(4,128)S(1)}, f32[3,1024]{1,0:T(4,128)S(1)}, u32[]{:S(2)}, u32[]{:S(2)}) collective-permute-start(f32[3,1024]{1,0:T(4,128)S(1)} %bitcast.141), channel_id=1, source_target_pairs={{8,0},{16,8},{24,16},{32,24},{40,32},{48,40},{56,48},{64,56},{72,6... | collective-permute-start | bytes 36872 | tf_op jit(solution)/shard_map/ppermute | solution.py:33
  21.4 6.0 %collective-permute-start.1 = (f32[10,2,1,2048]{3,0,2,1:T(8,128)S(1)}, f32[10,2,1,2048]{3,0,2,1:T(8,128)S(1)}, u32[]{:S(2)}, u32[]{:S(2)}) collective-permute-start(f32[10,2,1,2048]{3,0,2,1:T(8,128)S(1)} %copy.152), channel_id=1, source_target_pairs={{8,0},{16,8},{24,16},{32,24},{40,32},{48,40},{56,48},{64,56},{72,6... | collective-permute-start | bytes 491528 | tf_op jit(solution)/shard_map/ppermute | solution.py:23
  42.0 6.4 %collective-permute-start.19 = (f32[3,1024]{1,0:T(4,128)S(1)}, f32[3,1024]{1,0:T(4,128)S(1)}, u32[]{:S(2)}, u32[]{:S(2)}) collective-permute-start(f32[3,1024]{1,0:T(4,128)S(1)} %bitcast.137), channel_id=1, source_target_pairs={{8,0},{16,8},{24,16},{32,24},{40,32},{48,40},{56,48},{64,56},{72,6... | collective-permute-start | bytes 36872 | tf_op jit(solution)/shard_map/ppermute | solution.py:33
  54.2 4.7 copy.147
  58.9 6.2 %gather_fusion = f32[1024,10]{1,0:T(8,128)S(1)} fusion(f32[10,16384]{0,1:T(8,128)} %bitcast.120, s32[1024]{0:T(1024)S(1)} %fusion.316), kind=kCustom, calls=%fused_computation.clone | custom fusion | bytes 86016 | tf_op jit(solution)/shard_map/jit(_take)/gather | solution.py:160
  66.4 4.5 all-to-all-start.1
  72.9 6.0 %copy.136 = f32[10,2,4,2048]{0,2,1,3:T(4,128)} copy(f32[10,2,4,2048]{3,2,1,0:T(4,128)S(1)} %fusion.291) | data formatting | bytes 1310720 | tf_op jit(solution)/shard_map/add | solution.py:46
  78.9 12.2 %reshape.283 = f32[8,1,20480]{2,1,0:T(1,128)} reshape(f32[2048,2,4,10]{3,2,1,0:T(4,128)} %bitcast.116) | data formatting | bytes 1310720
  91.2 4.8 all-to-all-start
  100.1 7.6 %all-to-all-done = f32[8,1,20480]{2,1,0:T(1,128)S(1)} async-done(((f32[8,1,20480]{2,1,0:T(1,128)}), f32[8,1,20480]{2,1,0:T(1,128)S(1)}, u32[]{:S(2)}, u32[]{:S(2)}) %all-to-all-start) | async-done | bytes 655392 | tf_op jit(solution)/shard_map/all_to_all | solution.py:164
  110.5 14.6 %reshape.284 = f32[2048,2,4,10]{3,2,1,0:T(4,128)} reshape(f32[8,20480]{1,0:T(8,128)S(1)} %reduce.4) | data formatting | bytes 1310720
  125.1 7.2 %copy.137 = f32[10,2,4,8,256]{4,2,1,0,3:T(4,128)S(1)} copy(f32[10,2,4,8,256]{0,2,1,4,3:T(4,128)} %bitcast.117) | data formatting | bytes 1310720 | tf_op jit(solution)/shard_map/all_to_all | solution.py:164
  132.7 6.9 %fusion.370 = f32[1024,2048]{1,0:T(8,128)S(1)} fusion(f32[80,1024]{1,0:T(8,128)S(1)} %div.191, f32[80,2048]{1,0:T(8,128)S(1)} %reshape.255), kind=kOutput, calls=%fused_computation.410 | convolution fusion | flops 2013265920 | bytes 9371648 | tf_op jit(solution)/shard_map/dot_general | solution.py:70
  139.7 9.7 %fusion.144 = f32[80,2048]{1,0:T(8,128)S(1)} fusion(f32[80,1024]{1,0:T(8,128)S(1)} %get-tuple-element.11, f32[1024,2048]{1,0:T(8,128)S(1)} %fusion.370, f32[1024]{0:T(1024)S(1)} %bitcast.149, f32[2048]{0:T(1024)S(1)} %get-tuple-element.64, f32[1024]{0:T(1024)S(1)} %bitcast.148, f32[2048]{0:T(1024)S(1)} %fusion.311, f32[1024]{0:T(1024)S(1)} %bitcast.150, ...), kind=kOutput, calls=%fused_computation.146 | convolution fusion | flops 2044723200 | bytes 9408512 | tf_op jit(solution)/shard_map/dot_general | solution.py:87
  152.8 6.9 %fusion.374 = f32[1024,2048]{1,0:T(8,128)S(1)} fusion(f32[80,1024]{1,0:T(8,128)S(1)} %collective-permute-done.12, f32[80,2048]{1,0:T(8,128)S(1)} %reshape.255), kind=kOutput, calls=%fused_computation.414 | convolution fusion | flops 2013265920 | bytes 9371648 | tf_op jit(solution)/shard_map/dot_general | solution.py:70
  159.7 7.0 %collective-permute-done.11 = f32[80,1024]{1,0:T(8,128)S(1)} collective-permute-done((f32[80,1024]{1,0:T(8,128)S(1)}, f32[80,1024]{1,0:T(8,128)S(1)}, u32[]{:S(2)}, u32[]{:S(2)}) %collective-permute-start.11) | collective-permute-done | bytes 327712 | tf_op jit(solution)/shard_map/ppermute | solution.py:33
  168.9 9.5 %fusion.80 = f32[80,2048]{1,0:T(8,128)S(1)} fusion(f32[80,1024]{1,0:T(8,128)S(1)} %collective-permute-done.11, f32[1024,2048]{1,0:T(8,128)S(1)} %fusion.374, f32[1024]{0:T(1024)S(1)} %bitcast.155, f32[1024]{0:T(1024)S(1)} %bitcast.156, f32[1024]{0:T(1024)S(1)} %bitcast.154, f32[2048]{0:T(1024)S(1)} %get-tuple-element.64, f32[2048]{0:T(1024)S(1)} %fusion.311, ...), kind=kOutput, calls=%fused_computation.82 | convolution fusion | flops 2044723200 | bytes 9408512 | tf_op jit(solution)/shard_map/dot_general | solution.py:87
  178.4 9.8 %collective-permute-done.9 = f32[80,1024]{1,0:T(8,128)S(1)} collective-permute-done((f32[80,1024]{1,0:T(8,128)S(1)}, f32[80,1024]{1,0:T(8,128)S(1)}, u32[]{:S(2)}, u32[]{:S(2)}) %collective-permute-start.9) | collective-permute-done | bytes 327712 | tf_op jit(solution)/shard_map/ppermute | solution.py:33
  190.4 6.9 %fusion.373 = f32[1024,2048]{1,0:T(8,128)S(1)} fusion(f32[80,1024]{1,0:T(8,128)S(1)} %collective-permute-done.9, f32[80,2048]{1,0:T(8,128)S(1)} %reshape.255), kind=kOutput, calls=%fused_computation.413 | convolution fusion | flops 2013265920 | bytes 9371648 | tf_op jit(solution)/shard_map/dot_general | solution.py:70
  197.3 9.9 %collective-permute-done.8 = f32[80,1024]{1,0:T(8,128)S(1)} collective-permute-done((f32[80,1024]{1,0:T(8,128)S(1)}, f32[80,1024]{1,0:T(8,128)S(1)}, u32[]{:S(2)}, u32[]{:S(2)}) %collective-permute-start.8) | collective-permute-done | bytes 327712 | tf_op jit(solution)/shard_map/ppermute | solution.py:33
  209.6 9.5 %fusion.96 = f32[80,2048]{1,0:T(8,128)S(1)} fusion(f32[80,1024]{1,0:T(8,128)S(1)} %collective-permute-done.8, f32[1024,2048]{1,0:T(8,128)S(1)} %fusion.373, f32[1024]{0:T(1024)S(1)} %bitcast.152, f32[1024]{0:T(1024)S(1)} %bitcast.153, f32[1024]{0:T(1024)S(1)} %bitcast.151, f32[2048]{0:T(1024)S(1)} %get-tuple-element.64, f32[2048]{0:T(1024)S(1)} %fusion.311, ...), kind=kOutput, calls=%fused_computation.98 | convolution fusion | flops 2044723200 | bytes 9408512 | tf_op jit(solution)/shard_map/dot_general | solution.py:87
  221.9 6.9 %fusion.372 = f32[1024,2048]{1,0:T(8,128)S(1)} fusion(f32[80,1024]{1,0:T(8,128)S(1)} %collective-permute-done.6, f32[80,2048]{1,0:T(8,128)S(1)} %reshape.255), kind=kOutput, calls=%fused_computation.412 | convolution fusion | flops 2013265920 | bytes 9371648 | tf_op jit(solution)/shard_map/dot_general | solution.py:70
  233.2 9.5 %fusion.112 = f32[80,2048]{1,0:T(8,128)S(1)} fusion(f32[80,1024]{1,0:T(8,128)S(1)} %collective-permute-done.5, f32[1024,2048]{1,0:T(8,128)S(1)} %fusion.372, f32[1024]{0:T(1024)S(1)} %bitcast.173, f32[1024]{0:T(1024)S(1)} %bitcast.174, f32[1024]{0:T(1024)S(1)} %bitcast.172, f32[2048]{0:T(1024)S(1)} %get-tuple-element.64, f32[2048]{0:T(1024)S(1)} %fusion.311, ...), kind=kOutput, calls=%fused_computation.114 | convolution fusion | flops 2044723200 | bytes 9408512 | tf_op jit(solution)/shard_map/dot_general | solution.py:87
  246.2 6.9 %fusion.371 = f32[1024,2048]{1,0:T(8,128)S(1)} fusion(f32[80,1024]{1,0:T(8,128)S(1)} %collective-permute-done.3, f32[80,2048]{1,0:T(8,128)S(1)} %reshape.255), kind=kOutput, calls=%fused_computation.411 | convolution fusion | flops 2013265920 | bytes 9371648 | tf_op jit(solution)/shard_map/dot_general | solution.py:70
  253.8 9.8 %fusion.269 = f32[80,2048]{1,0:T(8,128)S(1)} fusion(f32[80,2048]{1,0:T(8,128)S(1)} %fusion.80, f32[80,2048]{1,0:T(8,128)S(1)} %fusion.96, f32[80,2048]{1,0:T(8,128)S(1)} %fusion.112, f32[80,2048]{1,0:T(8,128)S(1)} %fusion.144, f32[80,1024]{1,0:T(8,128)S(1)} %collective-permute-done.2, f32[1024,2048]{1,0:T(8,128)S(1)} %fusion.371, f32[1024]{0:T(1024)S(1)} %bitcast.164, ...), kind=kOutput, calls=%fused_computation.265 | convolution fusion | flops 2045378560 | bytes 12029952 | tf_op jit(solution)/shard_map/dot_general | solution.py:87
  269.3 11.0 %all-to-all-done.2 = f32[80,2,4,256]{3,2,1,0:T(4,128)S(1)} async-done(((f32[80,2,4,256]{3,2,1,0:T(4,128)}), f32[80,2,4,256]{3,2,1,0:T(4,128)S(1)}, u32[]{:S(2)}, u32[]{:S(2)}) %all-to-all-start.2) | async-done | bytes 655392 | tf_op jit(solution)/shard_map/all_to_all | solution.py:182
  280.3 4.7 copy.140
  285.0 6.2 %gather_fusion.1 = f32[1024,10]{1,0:T(8,128)S(1)} fusion(f32[10,16384]{0,1:T(8,128)} %bitcast.114, s32[1024]{0:T(1024)S(1)} %fusion.317), kind=kCustom, calls=%fused_computation.1.clone | custom fusion | bytes 86016 | tf_op jit(solution)/shard_map/jit(_take)/gather | solution.py:160
  296.5 12.0 %copy.141 = f32[10,2,4,8,256]{0,2,1,4,3:T(4,128)} copy(f32[10,2,4,8,256]{0,4,3,2,1:T(8,128)} %bitcast.115) | data formatting | bytes 1310720 | tf_op jit(solution)/shard_map/all_to_all | solution.py:182
  308.6 12.2 %reshape.285 = f32[8,1,20480]{2,1,0:T(1,128)} reshape(f32[2048,2,4,10]{3,2,1,0:T(4,128)} %bitcast.118) | data formatting | bytes 1310720
  320.8 4.7 all-to-all-start.3
  325.9 3.9 collective-permute-start.23
  332.6 6.0 %collective-permute-start.24 = (f32[80,1024]{1,0:T(8,128)S(1)}, f32[80,1024]{1,0:T(8,128)S(1)}, u32[]{:S(2)}, u32[]{:S(2)}) collective-permute-start(f32[80,1024]{1,0:T(8,128)S(1)} %get-tuple-element.8), channel_id=1, source_target_pairs={{16,0},{24,8},{32,16},{40,24},{48,32},{56,40},{64,48},{72,56},{80,... | collective-permute-start | bytes 983048 | tf_op jit(solution)/shard_map/ppermute | solution.py:33
  340.6 7.4 %collective-permute-start.17 = (f32[80,1024]{1,0:T(8,128)S(1)}, f32[80,1024]{1,0:T(8,128)}, u32[]{:S(2)}, u32[]{:S(2)}) collective-permute-start(f32[80,1024]{1,0:T(8,128)S(1)} %get-tuple-element.9), channel_id=1, source_target_pairs={{8,0},{16,8},{24,16},{32,24},{40,32},{48,40},{56,48},{64,56},{72,6... | collective-permute-start | bytes 983048 | tf_op jit(solution)/shard_map/ppermute | solution.py:33
  350.4 14.6 %reshape.286 = f32[2048,2,4,10]{3,2,1,0:T(4,128)} reshape(f32[8,20480]{1,0:T(8,128)S(1)} %reduce.5) | data formatting | bytes 1310720
  365.0 5.7 %copy.148 = f32[10,2,4,8,256]{4,3,2,1,0:T(8,128)S(1)} copy(f32[10,2,4,8,256]{0,2,1,4,3:T(4,128)} %bitcast.119) | data formatting | bytes 1310720 | tf_op jit(solution)/shard_map/all_to_all | solution.py:164
  371.3 6.9 %fusion.375 = f32[1024,2048]{1,0:T(8,128)S(1)} fusion(f32[80,1024]{1,0:T(8,128)S(1)} %div.220, f32[80,2048]{1,0:T(8,128)S(1)} %reshape.259), kind=kOutput, calls=%fused_computation.415 | convolution fusion | flops 2013265920 | bytes 9371648 | tf_op jit(solution)/shard_map/dot_general | solution.py:70
  378.3 9.7 %fusion.64 = f32[80,2048]{1,0:T(8,128)S(1)} fusion(f32[80,1024]{1,0:T(8,128)S(1)} %get-tuple-element.9, f32[1024,2048]{1,0:T(8,128)S(1)} %fusion.375, f32[1024]{0:T(1024)S(1)} %bitcast.146, f32[1024]{0:T(1024)S(1)} %bitcast.147, f32[1024]{0:T(1024)S(1)} %bitcast.145, f32[2048]{0:T(1024)S(1)} %get-tuple-element.64, f32[2048]{0:T(1024)S(1)} %fusion.311, ...), kind=kOutput, calls=%fused_computation.66 | convolution fusion | flops 2044723200 | bytes 9408512 | tf_op jit(solution)/shard_map/dot_general | solution.py:87
  390.2 6.9 %fusion.379 = f32[1024,2048]{1,0:T(8,128)S(1)} fusion(f32[80,1024]{1,0:T(8,128)S(1)} %collective-permute-done.24, f32[80,2048]{1,0:T(8,128)S(1)} %reshape.259), kind=kOutput, calls=%fused_computation.419 | convolution fusion | flops 2013265920 | bytes 9371648 | tf_op jit(solution)/shard_map/dot_general | solution.py:70
  401.0 10.5 %fusion = f32[80,2048]{1,0:T(8,128)S(1)} fusion(f32[80,1024]{1,0:T(8,128)} %collective-permute-done.23, f32[1024,2048]{1,0:T(8,128)S(1)} %fusion.379, f32[1024]{0:T(1024)S(1)} %bitcast.167, f32[1024]{0:T(1024)S(1)} %bitcast.168, f32[1024]{0:T(1024)S(1)} %bitcast.166, f32[2048]{0:T(1024)S(1)} %get-tuple-element.64, f32[2048]{0:T(1024)S(1)} %fusion.311, ...), kind=kOutput, calls=%fused_computation.2 | convolution fusion | flops 2044723200 | bytes 9408512 | tf_op jit(solution)/shard_map/dot_general | solution.py:87
  413.9 6.9 %fusion.378 = f32[1024,2048]{1,0:T(8,128)S(1)} fusion(f32[80,1024]{1,0:T(8,128)S(1)} %collective-permute-done.21, f32[80,2048]{1,0:T(8,128)S(1)} %reshape.259), kind=kOutput, calls=%fused_computation.418 | convolution fusion | flops 2013265920 | bytes 9371648 | tf_op jit(solution)/shard_map/dot_general | solution.py:70
  420.9 10.7 %fusion.16 = f32[80,2048]{1,0:T(8,128)S(1)} fusion(f32[80,1024]{1,0:T(8,128)} %collective-permute-done.20, f32[1024,2048]{1,0:T(8,128)S(1)} %fusion.378, f32[1024]{0:T(1024)S(1)} %bitcast.158, f32[1024]{0:T(1024)S(1)} %bitcast.159, f32[1024]{0:T(1024)S(1)} %bitcast.157, f32[2048]{0:T(1024)S(1)} %get-tuple-element.64, f32[2048]{0:T(1024)S(1)} %fusion.311, ...), kind=kOutput, calls=%fused_computation.18 | convolution fusion | flops 2044723200 | bytes 9408512 | tf_op jit(solution)/shard_map/dot_general | solution.py:87
  431.6 6.9 %fusion.377 = f32[1024,2048]{1,0:T(8,128)S(1)} fusion(f32[80,1024]{1,0:T(8,128)S(1)} %collective-permute-done.18, f32[80,2048]{1,0:T(8,128)S(1)} %reshape.259), kind=kOutput, calls=%fused_computation.417 | convolution fusion | flops 2013265920 | bytes 9371648 | tf_op jit(solution)/shard_map/dot_general | solution.py:70
  438.5 10.7 %fusion.32 = f32[80,2048]{1,0:T(8,128)S(1)} fusion(f32[80,1024]{1,0:T(8,128)} %collective-permute-done.17, f32[1024,2048]{1,0:T(8,128)S(1)} %fusion.377, f32[1024]{0:T(1024)S(1)} %bitcast.170, f32[1024]{0:T(1024)S(1)} %bitcast.171, f32[1024]{0:T(1024)S(1)} %bitcast.169, f32[2048]{0:T(1024)S(1)} %get-tuple-element.64, f32[2048]{0:T(1024)S(1)} %fusion.311, ...), kind=kOutput, calls=%fused_computation.34 | convolution fusion | flops 2044723200 | bytes 9408512 | tf_op jit(solution)/shard_map/dot_general | solution.py:87
  449.3 7.2 %fusion.376 = f32[1024,2048]{1,0:T(8,128)S(1)} fusion(f32[80,1024]{1,0:T(8,128)S(1)} %collective-permute-done.15, f32[80,2048]{1,0:T(8,128)S(1)} %reshape.259), kind=kOutput, calls=%fused_computation.416 | convolution fusion | flops 2013265920 | bytes 9371648 | tf_op jit(solution)/shard_map/dot_general | solution.py:70
  456.5 9.6 %fusion.281 = f32[80,2048]{1,0:T(8,128)S(1)} fusion(f32[80,2048]{1,0:T(8,128)S(1)} %fusion, f32[80,2048]{1,0:T(8,128)S(1)} %fusion.16, f32[80,2048]{1,0:T(8,128)S(1)} %fusion.32, f32[80,2048]{1,0:T(8,128)S(1)} %fusion.64, f32[80,1024]{1,0:T(8,128)S(1)} %collective-permute-done.14, f32[1024,2048]{1,0:T(8,128)S(1)} %fusion.376, f32[1024]{0:T(1024)S(1)} %bitcast.161, ...), kind=kOutput, calls=%fused_computation.269 | convolution fusion | flops 2045378560 | bytes 12029952 | tf_op jit(solution)/shard_map/dot_general | solution.py:87
  466.8 16.4 %all_to_all.82 = f32[80,2,4,256]{3,2,1,0:T(4,128)S(1)} all-to-all(f32[80,2,4,256]{3,2,1,0:T(4,128)S(1)} %bitcast_add_fusion.1), channel_id=1, replica_groups=mesh['tile'=32,'ens'=8] {'ens'}, dimensions={0} | all-to-all | bytes 1310720 | tf_op jit(solution)/shard_map/all_to_all | solution.py:182
  (118 shorter events, 87.2 us)
Async XLA Ops:
  0.9 30.5 %collective-permute-start.13 = (f32[3,1024]{1,0:T(4,128)S(1)}, f32[3,1024]{1,0:T(4,128)S(1)}, u32[]{:S(2)}, u32[]{:S(2)}) collective-permute-start(f32[3,1024]{1,0:T(4,128)S(1)} %bitcast.139), channel_id=1, source_target_pairs={{16,0},{24,8},{32,16},{40,24},{48,32},{56,40},{64,48},{72,56},{80,... | collective-permute-start | bytes 36872 | tf_op jit(solution)/shard_map/ppermute | solution.py:33
  9.3 24.0 %collective-permute-start.10 = (f32[3,1024]{1,0:T(4,128)S(1)}, f32[3,1024]{1,0:T(4,128)S(1)}, u32[]{:S(2)}, u32[]{:S(2)}) collective-permute-start(f32[3,1024]{1,0:T(4,128)S(1)} %bitcast.140), channel_id=1, source_target_pairs={{0,16},{8,24},{16,32},{24,40},{32,48},{40,56},{48,64},{56,72},{64,... | collective-permute-start | bytes 36872 | tf_op jit(solution)/shard_map/ppermute | solution.py:33
  11.3 59.6 %collective-permute-start.7 = (f32[3,1024]{1,0:T(4,128)S(1)}, f32[3,1024]{1,0:T(4,128)S(1)}, u32[]{:S(2)}, u32[]{:S(2)}) collective-permute-start(f32[3,1024]{1,0:T(4,128)S(1)} %bitcast.141), channel_id=1, source_target_pairs={{8,0},{16,8},{24,16},{32,24},{40,32},{48,40},{56,48},{64,56},{72,6... | collective-permute-start | bytes 36872 | tf_op jit(solution)/shard_map/ppermute | solution.py:33
  17.8 55.1 %collective-permute-start.4 = (f32[3,1024]{1,0:T(4,128)S(1)}, f32[3,1024]{1,0:T(4,128)S(1)}, u32[]{:S(2)}, u32[]{:S(2)}) collective-permute-start(f32[3,1024]{1,0:T(4,128)S(1)} %bitcast.142), channel_id=1, source_target_pairs={{0,8},{8,16},{16,24},{24,32},{32,40},{40,48},{48,56},{56,64},{64,7... | collective-permute-start | bytes 36872 | tf_op jit(solution)/shard_map/ppermute | solution.py:33
  21.4 15.3 %collective-permute-start.1 = (f32[10,2,1,2048]{3,0,2,1:T(8,128)S(1)}, f32[10,2,1,2048]{3,0,2,1:T(8,128)S(1)}, u32[]{:S(2)}, u32[]{:S(2)}) collective-permute-start(f32[10,2,1,2048]{3,0,2,1:T(8,128)S(1)} %copy.152), channel_id=1, source_target_pairs={{8,0},{16,8},{24,16},{32,24},{40,32},{48,40},{56,48},{64,56},{72,6... | collective-permute-start | bytes 491528 | tf_op jit(solution)/shard_map/ppermute | solution.py:23
  31.4 10.6 %collective-permute-start = (f32[10,2,1,2048]{3,0,2,1:T(8,128)S(1)}, f32[10,2,1,2048]{3,0,2,1:T(8,128)S(1)}, u32[]{:S(2)}, u32[]{:S(2)}) collective-permute-start(f32[10,2,1,2048]{3,0,2,1:T(8,128)S(1)} %copy.151), channel_id=1, source_target_pairs={{0,8},{8,16},{16,24},{24,32},{32,40},{40,48},{48,56},{56,64},{64,7... | collective-permute-start | bytes 491528 | tf_op jit(solution)/shard_map/ppermute | solution.py:21
  33.3 235.9 %collective-permute-start.25 = (f32[3,1024]{1,0:T(4,128)S(1)}, f32[3,1024]{1,0:T(4,128)S(1)}, u32[]{:S(2)}, u32[]{:S(2)}) collective-permute-start(f32[3,1024]{1,0:T(4,128)S(1)} %bitcast.135), channel_id=1, source_target_pairs={{16,0},{24,8},{32,16},{40,24},{48,32},{56,40},{64,48},{72,56},{80,... | collective-permute-start | bytes 36872 | tf_op jit(solution)/shard_map/ppermute | solution.py:33
  36.8 232.5 %collective-permute-start.22 = (f32[3,1024]{1,0:T(4,128)S(1)}, f32[3,1024]{1,0:T(4,128)S(1)}, u32[]{:S(2)}, u32[]{:S(2)}) collective-permute-start(f32[3,1024]{1,0:T(4,128)S(1)} %bitcast.136), channel_id=1, source_target_pairs={{0,16},{8,24},{16,32},{24,40},{32,48},{40,56},{48,64},{56,72},{64,... | collective-permute-start | bytes 36872 | tf_op jit(solution)/shard_map/ppermute | solution.py:33
  42.0 253.9 %collective-permute-start.19 = (f32[3,1024]{1,0:T(4,128)S(1)}, f32[3,1024]{1,0:T(4,128)S(1)}, u32[]{:S(2)}, u32[]{:S(2)}) collective-permute-start(f32[3,1024]{1,0:T(4,128)S(1)} %bitcast.137), channel_id=1, source_target_pairs={{8,0},{16,8},{24,16},{32,24},{40,32},{48,40},{56,48},{64,56},{72,6... | collective-permute-start | bytes 36872 | tf_op jit(solution)/shard_map/ppermute | solution.py:33
  66.4 24.8 %all-to-all-start.1 = ((f32[8,10,1024]{2,1,0:T(8,128)}), f32[8,10,1024]{2,1,0:T(8,128)S(1)}, u32[]{:S(2)}, u32[]{:S(2)}) async-start(f32[8,10,1024]{2,1,0:T(8,128)} %stack.4), calls=%async_computation.1 | async-start | bytes 1048576 | tf_op jit(solution)/shard_map/all_to_all | solution.py:162
  70.9 225.6 %collective-permute-start.16 = (f32[3,1024]{1,0:T(4,128)S(1)}, f32[3,1024]{1,0:T(4,128)S(1)}, u32[]{:S(2)}, u32[]{:S(2)}) collective-permute-start(f32[3,1024]{1,0:T(4,128)S(1)} %bitcast.138), channel_id=1, source_target_pairs={{0,8},{8,16},{16,24},{24,32},{32,40},{40,48},{48,56},{56,64},{64,7... | collective-permute-start | bytes 36872 | tf_op jit(solution)/shard_map/ppermute | solution.py:33
  72.9 23.3 %copy-start = (f32[2,1024]{1,0:T(2,128)S(1)}, f32[2,1024]{1,0:T(2,128)}, u32[]{:S(2)}) copy-start(f32[2,1024]{1,0:T(2,128)} %param.13) | copy-start | bytes 24580
  72.9 23.3 %copy-start.1 = (f32[2,1024]{1,0:T(2,128)S(1)}, f32[2,1024]{1,0:T(2,128)}, u32[]{:S(2)}) copy-start(f32[2,1024]{1,0:T(2,128)} %param.12) | copy-start | bytes 24580
  91.2 16.5 %all-to-all-start = ((f32[8,1,20480]{2,1,0:T(1,128)}), f32[8,1,20480]{2,1,0:T(1,128)S(1)}, u32[]{:S(2)}, u32[]{:S(2)}) async-start(f32[8,1,20480]{2,1,0:T(1,128)} %reshape.283), calls=%async_computation | async-start | bytes 1310720 | tf_op jit(solution)/shard_map/all_to_all | solution.py:164
  96.3 53.0 %collective-permute-start.12 = (f32[80,1024]{1,0:T(8,128)S(1)}, f32[80,1024]{1,0:T(8,128)S(1)}, u32[]{:S(2)}, u32[]{:S(2)}) collective-permute-start(f32[80,1024]{1,0:T(8,128)S(1)} %get-tuple-element.10), channel_id=1, source_target_pairs={{16,0},{24,8},{32,16},{40,24},{48,32},{56,40},{64,48},{72,56},{80,... | collective-permute-start | bytes 983048 | tf_op jit(solution)/shard_map/ppermute | solution.py:33
  149.4 17.3 %collective-permute-start.11 = (f32[80,1024]{1,0:T(8,128)S(1)}, f32[80,1024]{1,0:T(8,128)S(1)}, u32[]{:S(2)}, u32[]{:S(2)}) collective-permute-start(f32[80,1024]{1,0:T(8,128)S(1)} %get-tuple-element.11), channel_id=1, source_target_pairs={{16,0},{24,8},{32,16},{40,24},{48,32},{56,40},{64,48},{72,56},{80,... | collective-permute-start | bytes 983048 | tf_op jit(solution)/shard_map/ppermute | solution.py:33
  166.7 21.5 %collective-permute-start.9 = (f32[80,1024]{1,0:T(8,128)S(1)}, f32[80,1024]{1,0:T(8,128)S(1)}, u32[]{:S(2)}, u32[]{:S(2)}) collective-permute-start(f32[80,1024]{1,0:T(8,128)S(1)} %get-tuple-element.10), channel_id=1, source_target_pairs={{0,16},{8,24},{16,32},{24,40},{32,48},{40,56},{48,64},{56,72},{64,... | collective-permute-start | bytes 983048 | tf_op jit(solution)/shard_map/ppermute | solution.py:33
  188.2 19.0 %collective-permute-start.8 = (f32[80,1024]{1,0:T(8,128)S(1)}, f32[80,1024]{1,0:T(8,128)S(1)}, u32[]{:S(2)}, u32[]{:S(2)}) collective-permute-start(f32[80,1024]{1,0:T(8,128)S(1)} %get-tuple-element.11), channel_id=1, source_target_pairs={{0,16},{8,24},{16,32},{24,40},{32,48},{40,56},{48,64},{56,72},{64,... | collective-permute-start | bytes 983048 | tf_op jit(solution)/shard_map/ppermute | solution.py:33
  207.2 11.9 %collective-permute-start.6 = (f32[80,1024]{1,0:T(8,128)S(1)}, f32[80,1024]{1,0:T(8,128)S(1)}, u32[]{:S(2)}, u32[]{:S(2)}) collective-permute-start(f32[80,1024]{1,0:T(8,128)S(1)} %get-tuple-element.10), channel_id=1, source_target_pairs={{8,0},{16,8},{24,16},{32,24},{40,32},{48,40},{56,48},{64,56},{72,6... | collective-permute-start | bytes 983048 | tf_op jit(solution)/shard_map/ppermute | solution.py:33
  219.2 10.2 %collective-permute-start.5 = (f32[80,1024]{1,0:T(8,128)S(1)}, f32[80,1024]{1,0:T(8,128)S(1)}, u32[]{:S(2)}, u32[]{:S(2)}) collective-permute-start(f32[80,1024]{1,0:T(8,128)S(1)} %get-tuple-element.11), channel_id=1, source_target_pairs={{8,0},{16,8},{24,16},{32,24},{40,32},{48,40},{56,48},{64,56},{72,6... | collective-permute-start | bytes 983048 | tf_op jit(solution)/shard_map/ppermute | solution.py:33
  229.3 13.4 %collective-permute-start.3 = (f32[80,1024]{1,0:T(8,128)S(1)}, f32[80,1024]{1,0:T(8,128)S(1)}, u32[]{:S(2)}, u32[]{:S(2)}) collective-permute-start(f32[80,1024]{1,0:T(8,128)S(1)} %get-tuple-element.10), channel_id=1, source_target_pairs={{0,8},{8,16},{16,24},{24,32},{32,40},{40,48},{48,56},{56,64},{64,7... | collective-permute-start | bytes 983048 | tf_op jit(solution)/shard_map/ppermute | solution.py:33
  242.7 11.1 %collective-permute-start.2 = (f32[80,1024]{1,0:T(8,128)S(1)}, f32[80,1024]{1,0:T(8,128)S(1)}, u32[]{:S(2)}, u32[]{:S(2)}) collective-permute-start(f32[80,1024]{1,0:T(8,128)S(1)} %get-tuple-element.11), channel_id=1, source_target_pairs={{0,8},{8,16},{16,24},{24,32},{32,40},{40,48},{48,56},{56,64},{64,7... | collective-permute-start | bytes 983048 | tf_op jit(solution)/shard_map/ppermute | solution.py:33
  265.1 15.2 %all-to-all-start.2 = ((f32[80,2,4,256]{3,2,1,0:T(4,128)}), f32[80,2,4,256]{3,2,1,0:T(4,128)S(1)}, u32[]{:S(2)}, u32[]{:S(2)}) async-start(f32[80,2,4,256]{3,2,1,0:T(4,128)} %bitcast_add_fusion), calls=%async_computation.2 | async-start | bytes 1310720 | tf_op jit(solution)/shard_map/all_to_all | solution.py:182
  292.4 28.4 %all-to-all-start.4 = ((f32[8,10,1024]{2,1,0:T(8,128)}), f32[8,10,1024]{2,1,0:T(8,128)S(1)}, u32[]{:S(2)}, u32[]{:S(2)}) async-start(f32[8,10,1024]{2,1,0:T(8,128)} %stack.5), calls=%async_computation.4 | async-start | bytes 1048576 | tf_op jit(solution)/shard_map/all_to_all | solution.py:162
  320.8 27.4 %all-to-all-start.3 = ((f32[8,1,20480]{2,1,0:T(1,128)}), f32[8,1,20480]{2,1,0:T(1,128)S(1)}, u32[]{:S(2)}, u32[]{:S(2)}) async-start(f32[8,1,20480]{2,1,0:T(1,128)} %reshape.285), calls=%async_computation.3 | async-start | bytes 1310720 | tf_op jit(solution)/shard_map/all_to_all | solution.py:164
  325.9 71.3 %collective-permute-start.23 = (f32[80,1024]{1,0:T(8,128)S(1)}, f32[80,1024]{1,0:T(8,128)}, u32[]{:S(2)}, u32[]{:S(2)}) collective-permute-start(f32[80,1024]{1,0:T(8,128)S(1)} %get-tuple-element.9), channel_id=1, source_target_pairs={{16,0},{24,8},{32,16},{40,24},{48,32},{56,40},{64,48},{72,56},{80,... | collective-permute-start | bytes 983048 | tf_op jit(solution)/shard_map/ppermute | solution.py:33
  329.8 91.0 %collective-permute-start.20 = (f32[80,1024]{1,0:T(8,128)S(1)}, f32[80,1024]{1,0:T(8,128)}, u32[]{:S(2)}, u32[]{:S(2)}) collective-permute-start(f32[80,1024]{1,0:T(8,128)S(1)} %get-tuple-element.9), channel_id=1, source_target_pairs={{0,16},{8,24},{16,32},{24,40},{32,48},{40,56},{48,64},{56,72},{64,... | collective-permute-start | bytes 983048 | tf_op jit(solution)/shard_map/ppermute | solution.py:33
  332.6 55.4 %collective-permute-start.24 = (f32[80,1024]{1,0:T(8,128)S(1)}, f32[80,1024]{1,0:T(8,128)S(1)}, u32[]{:S(2)}, u32[]{:S(2)}) collective-permute-start(f32[80,1024]{1,0:T(8,128)S(1)} %get-tuple-element.8), channel_id=1, source_target_pairs={{16,0},{24,8},{32,16},{40,24},{48,32},{56,40},{64,48},{72,56},{80,... | collective-permute-start | bytes 983048 | tf_op jit(solution)/shard_map/ppermute | solution.py:33
  338.7 72.9 %collective-permute-start.21 = (f32[80,1024]{1,0:T(8,128)S(1)}, f32[80,1024]{1,0:T(8,128)S(1)}, u32[]{:S(2)}, u32[]{:S(2)}) collective-permute-start(f32[80,1024]{1,0:T(8,128)S(1)} %get-tuple-element.8), channel_id=1, source_target_pairs={{0,16},{8,24},{16,32},{24,40},{32,48},{40,56},{48,64},{56,72},{64,... | collective-permute-start | bytes 983048 | tf_op jit(solution)/shard_map/ppermute | solution.py:33
  340.6 97.9 %collective-permute-start.17 = (f32[80,1024]{1,0:T(8,128)S(1)}, f32[80,1024]{1,0:T(8,128)}, u32[]{:S(2)}, u32[]{:S(2)}) collective-permute-start(f32[80,1024]{1,0:T(8,128)S(1)} %get-tuple-element.9), channel_id=1, source_target_pairs={{8,0},{16,8},{24,16},{32,24},{40,32},{48,40},{56,48},{64,56},{72,6... | collective-permute-start | bytes 983048 | tf_op jit(solution)/shard_map/ppermute | solution.py:33
  388.0 43.6 %collective-permute-start.18 = (f32[80,1024]{1,0:T(8,128)S(1)}, f32[80,1024]{1,0:T(8,128)S(1)}, u32[]{:S(2)}, u32[]{:S(2)}) collective-permute-start(f32[80,1024]{1,0:T(8,128)S(1)} %get-tuple-element.8), channel_id=1, source_target_pairs={{8,0},{16,8},{24,16},{32,24},{40,32},{48,40},{56,48},{64,56},{72,6... | collective-permute-start | bytes 983048 | tf_op jit(solution)/shard_map/ppermute | solution.py:33
  397.2 59.3 %collective-permute-start.14 = (f32[80,1024]{1,0:T(8,128)S(1)}, f32[80,1024]{1,0:T(8,128)S(1)}, u32[]{:S(2)}, u32[]{:S(2)}) collective-permute-start(f32[80,1024]{1,0:T(8,128)S(1)} %get-tuple-element.9), channel_id=1, source_target_pairs={{0,8},{8,16},{16,24},{24,32},{32,40},{40,48},{48,56},{56,64},{64,7... | collective-permute-start | bytes 983048 | tf_op jit(solution)/shard_map/ppermute | solution.py:33
  411.6 37.7 %collective-permute-start.15 = (f32[80,1024]{1,0:T(8,128)S(1)}, f32[80,1024]{1,0:T(8,128)S(1)}, u32[]{:S(2)}, u32[]{:S(2)}) collective-permute-start(f32[80,1024]{1,0:T(8,128)S(1)} %get-tuple-element.8), channel_id=1, source_target_pairs={{0,8},{8,16},{16,24},{24,32},{32,40},{40,48},{48,56},{56,64},{64,7... | collective-permute-start | bytes 983048 | tf_op jit(solution)/shard_map/ppermute | solution.py:33
  431.5 7.0 %copy-start.2 = (f32[1,1024]{1,0:T(1,128)S(1)}, f32[1,1024]{1,0:T(1,128)}, u32[]{:S(2)}) copy-start(f32[1,1024]{1,0:T(1,128)} %get-tuple-element.25) | copy-start | bytes 12292
